TPU v7x, 32 devices: a whole 2x2x4 slice. The times are simulated.
32 devices in a mesh: mode: 8 (over z, y), rep: 4 (over x, core).
Axes of the slice: x: 2, y: 2, z: 4, core: 2. Of those that a mesh axis runs over, the one named last changes fastest.
Arguments:
- first_cores: float32 [2, 8, 128, 64], P(None, 'rep', 'mode'), may hold values from -6 to 6
- mid_cores: float32 [2, 8, 3, 128, 4096], P(None, 'rep', None, 'mode'), may hold values from -2 to 2
- last_cores: float32 [2, 8, 128, 64], P(None, 'rep', 'mode'), may hold values from -0.75 to 0.75
- sketch_mid: float32 [3, 128, 4096], P(None, 'mode'), may hold values from -0.0625 to 0.0625
- sketch_last: float32 [128, 64], P('mode'), may hold values from -0.5 to 0.5
- ranks: int32 [4], replicated, may hold values from 32 to 64, as said below
Outputs:
- rounded_first: float32 [2, 128, 64], P(None, 'mode')
- rounded_mid: float32 [2, 3, 128, 4096], P(None, None, 'mode')
- rounded_last: float32 [2, 128, 64], P(None, 'mode')
Inputs may be any that keep to these rules, and one draw needn't show every extreme that they name: `ranks`: some bond has rank 64.
All inputs are finite; a program needn't handle non-finite values.
Results may differ from a plain program's by a relative error of at most 0.00019.
Values sent between devices are 32-bit elements; how exact they have to be, the bound alone decides.
No kernel may reach another device: no remote copies, remote signals or barrier semaphores. Data moves between devices by JAX's collectives and lax.ppermute only.
A program may use at most 64 MiB of HBM per device.

v0:
```python
import jax
import jax.numpy as jnp
from jax import lax
from jax.sharding import PartitionSpec as P

PRECISE = lax.Precision.HIGHEST


def lower_inverse(gram_matrix):
    factor = jnp.linalg.cholesky(gram_matrix)
    identity = jnp.eye(gram_matrix.shape[-1], dtype=gram_matrix.dtype)
    return jax.vmap(lambda single: jax.scipy.linalg.solve_triangular(single, identity, lower=True))(
        factor
    )


def sketch_total(partial_value):
    return lax.psum(partial_value, "mode")


def orthogonal(pieces, sketch, bond_mask, row_count):
    local_mix = jnp.einsum("bsiad,bsde->biae", pieces, sketch, precision=PRECISE)
    mixture = lax.psum(local_mix, "rep")
    gram_part = jnp.einsum("biae,biaf->bef", mixture, mixture, precision=PRECISE)
    raw_part = jnp.einsum("biae,bsiad->bsed", mixture, pieces, precision=PRECISE)
    gram_total, raw_total = lax.psum((gram_part, raw_part), "mode")
    inverse = lower_inverse(gram_total / row_count + jnp.diag(1.0 - bond_mask))
    ortho_basis = jnp.einsum("biae,bfe->biaf", mixture, inverse, precision=PRECISE)
    carried = jnp.einsum("bfe,bsed->bsfd", inverse, raw_total, precision=PRECISE) / row_count
    return (ortho_basis, carried)


def per_device(first_cores, mid_cores, last_cores, sketch_mid, sketch_last, ranks):
    members, summands, slices, rank_size = first_cores.shape
    middle = mid_cores.shape[2]
    total_slices = slices * lax.axis_size("mode")
    bond_masks = (jnp.arange(rank_size, dtype=jnp.int32)[None, :] < ranks[:, None]).astype(
        jnp.float32
    )
    middle_cores = mid_cores.reshape(members, summands, middle, slices, rank_size, rank_size)
    sketch_cores = sketch_mid.reshape(middle, slices, rank_size, rank_size)
    newest = (
        sketch_total(jnp.einsum("bsic,ie->bsce", last_cores, sketch_last, precision=PRECISE))
        * bond_masks[middle]
    )
    stored = jnp.zeros((middle + 1, members, summands, rank_size, rank_size), jnp.float32)
    stored = stored.at[middle].set(newest)

    def right_step(step, sketches):
        position = middle - 1 - step
        current = lax.dynamic_index_in_dim(sketches, position + 1, 0, keepdims=False)
        core_now = lax.dynamic_index_in_dim(middle_cores, position, 2, keepdims=False)
        sketch_now = lax.dynamic_index_in_dim(sketch_cores, position, 0, keepdims=False)
        mask_now = lax.dynamic_index_in_dim(bond_masks, position, 0, keepdims=False)
        partial_value = jnp.einsum("bsicd,bsde->bsice", core_now, current, precision=PRECISE)
        folded = jnp.einsum("bsice,ife->bscf", partial_value, sketch_now, precision=PRECISE)
        updated = sketch_total(folded) * mask_now
        return lax.dynamic_update_index_in_dim(sketches, updated, position, 0)

    stored = lax.fori_loop(0, middle, right_step, stored)
    pieces = first_cores[:, :, :, None, :]
    ortho_basis, carried = orthogonal(pieces, stored[0], bond_masks[0], total_slices)
    rounded_first = ortho_basis[:, :, 0, :]
    buffer = jnp.zeros((members, middle, slices, rank_size * rank_size), jnp.float32)

    def left_step(position, state):
        carried_now, buffer_now = state
        core_now = lax.dynamic_index_in_dim(middle_cores, position, 2, keepdims=False)
        sketch_now = lax.dynamic_index_in_dim(stored, position + 1, 0, keepdims=False)
        mask_now = lax.dynamic_index_in_dim(bond_masks, position + 1, 0, keepdims=False)
        pieces_now = jnp.einsum("bsac,bsicd->bsiad", carried_now, core_now, precision=PRECISE)
        basis_now, carried_next = orthogonal(
            pieces_now, sketch_now, mask_now, total_slices * rank_size
        )
        flat_basis = basis_now.reshape(members, slices, rank_size * rank_size)
        buffer_next = lax.dynamic_update_index_in_dim(buffer_now, flat_basis, position, 1)
        return (carried_next, buffer_next)

    carried, rounded_mid = lax.fori_loop(0, middle, left_step, (carried, buffer))
    local_last = jnp.einsum("bsac,bsic->bia", carried, last_cores, precision=PRECISE)
    rounded_last = lax.psum(local_last, "rep")
    return (rounded_first, rounded_mid, rounded_last)


def solution(mesh):
    return jax.shard_map(
        per_device,
        mesh=mesh,
        in_specs=(
            P(None, "rep", "mode", None),
            P(None, "rep", None, "mode", None),
            P(None, "rep", "mode", None),
            P(None, "mode", None),
            P("mode", None),
            P(),
        ),
        out_specs=(P(None, "mode", None), P(None, None, "mode", None), P(None, "mode", None)),
        check_vma=False,
    )
```

profile of v0, /device:TPU:0, one launch (start us, length us, event | category | flops | bytes accessed | tf_op | source)
XLA Modules:
  0.0 836.8 jit_solution(11274654828225337695)
XLA Ops:
  9.8 6.2 reshape.148
  16.8 67.7 %all-reduce.7.cloned.1.call-done = f32[2,2,64,64]{3,2,1,0:T(8,128)} async-done(((f32[2,2,64,64]{3,2,1,0:T(8,128)}), f32[2,2,64,64]{3,2,1,0:T(8,128)}) %all-reduce.7.cloned.1.call-update) | async-done | bytes 65552 | tf_op jit(solution)/shard_map/psum | solution.py:18
  85.4 229.9 %while.35 = (s32[]{:T(128)}, f32[4,2,2,64,64]{4,3,2,1,0:T(8,128)S(1)}, f32[2,2,3,16,64,64]{5,4,3,2,1,0:T(8,128)}, f32[3,16,64,64]{3,2,1,0:T(8,128)S(1)}, f32[4,6...) while((s32[]{:T(128)}, ...), condition=%wide.region_3.4_spmd, body=%wide.region_1.3_spmd.sunk | while | flops 402685952 | bytes 6685998 | solution.py:60
  91.5 69.6 %all-reduce.11.cloned.1.call-done = f32[2,2,64,64]{3,2,1,0:T(8,128)} async-done(((f32[2,2,64,64]{3,2,1,0:T(8,128)}), f32[2,2,64,64]{3,2,1,0:T(8,128)}) %all-reduce.11.cloned.1.call-update) | async-done | bytes 65552 | tf_op jit(solution)/shard_map/while/body/eval_jaxpr/psum | solution.py:18
  168.2 69.6 %all-reduce.11.cloned.1.call-done = f32[2,2,64,64]{3,2,1,0:T(8,128)} async-done(((f32[2,2,64,64]{3,2,1,0:T(8,128)}), f32[2,2,64,64]{3,2,1,0:T(8,128)}) %all-reduce.11.cloned.1.call-update) | async-done | bytes 65552 | tf_op jit(solution)/shard_map/while/body/eval_jaxpr/psum | solution.py:18
  244.8 69.6 %all-reduce.11.cloned.1.call-done = f32[2,2,64,64]{3,2,1,0:T(8,128)} async-done(((f32[2,2,64,64]{3,2,1,0:T(8,128)}), f32[2,2,64,64]{3,2,1,0:T(8,128)}) %all-reduce.11.cloned.1.call-update) | async-done | bytes 65552 | tf_op jit(solution)/shard_map/while/body/eval_jaxpr/psum | solution.py:18
  315.6 10.1 %psum.95 = f32[2,16,64]{2,1,0:T(8,128)S(1)} all-reduce(f32[2,16,64]{2,1,0:T(8,128)S(1)} %convolution_bitcast_fusion.5), channel_id=1, replica_groups=mesh['mode'=8,'rep'=4] {'rep'}, use_global_device_ids=true, to_apply=%region_4.5 | all-reduce | flops 2048 | bytes 16384 | tf_op jit(solution)/shard_map/psum | solution.py:23
  327.0 35.7 %psum.96 = f32[2,64,64]{1,2,0:T(8,128)S(1)} all-reduce(f32[2,64,64]{1,2,0:T(8,128)S(1)} %fusion.52), channel_id=1, replica_groups=mesh['mode'=8,'rep'=4] {'mode'}, use_global_device_ids=true, to_apply=%region_5.6 | all-reduce | flops 8192 | bytes 65536 | tf_op jit(solution)/shard_map/psum | solution.py:26
  362.8 11.7 %custom-call.10 = f32[2,64,64]{2,1,0:T(8,128)S(1)} custom-call(f32[2,64,64]{2,1,0:T(8,128)S(1)} %fusion.43), custom_call_target="Cholesky" | custom-call | tf_op jit(solution)/shard_map/jit(cholesky)/cholesky | solution.py:10
  374.8 9.8 %custom-call.11 = f32[2,1,64,64]{2,3,1,0:T(8,128)S(1)} custom-call(f32[2,1,64,64]{3,2,1,0:T(8,128)S(1)} %select_bitcast_fusion.1), custom_call_target="InvertDiagBlocksLowerTriangular" | custom-call | tf_op jit(solution)/shard_map/vmap(jit(_solve_triangular))/triangular_solve | solution.py:12
  385.8 66.8 %all-reduce.9.cloned.1.call-done = f32[2,2,64,64]{3,2,1,0:T(8,128)} async-done(((f32[2,2,64,64]{3,2,1,0:T(8,128)}), f32[2,2,64,64]{3,2,1,0:T(8,128)}) %all-reduce.9.cloned.1.call-update) | async-done | bytes 65552 | tf_op jit(solution)/shard_map/psum | solution.py:26
  453.9 365.3 %while.36 = (s32[]{:T(128)}, f32[2,2,64,64]{2,3,1,0:T(8,128)S(1)}, f32[2,3,16,4096]{3,2,1,0:T(8,128)}, f32[2,2,3,16,64,64]{5,4,3,2,1,0:T(8,128)}, f32[4,2,2,64,6...) while((s32[]{:T(128)}, f32[2,2,64,64]{2,3,1,0:T(8,128)S(1)}, ...), condition=%wide.region_13.16_spmd, body=%wide.region_9.15_spmd.sunk | while | flops 824467648 | bytes 21006400 | solution.py:79
  454.2 5.1 fusion.120
  459.4 4.4 fusion.121
  464.0 35.3 %all-reduce.13.cloned.1.call-done = f32[2,16,64,64]{3,2,1,0:T(8,128)} async-done(((f32[2,16,64,64]{3,2,1,0:T(8,128)}), f32[2,16,64,64]{3,2,1,0:T(8,128)}) %all-reduce.13.cloned.1.call-update) | async-done | bytes 524304 | tf_op jit(solution)/shard_map/while/body/eval_jaxpr/psum | solution.py:23
  505.1 37.6 %psum.106 = f32[2,64,64]{1,2,0:T(8,128)S(1)} all-reduce(f32[2,64,64]{1,2,0:T(8,128)S(1)} %convolution_bitcast_fusion.10), channel_id=1, replica_groups=mesh['mode'=8,'rep'=4] {'mode'}, use_global_device_ids=true, to_apply=%region_12.14 | all-reduce | flops 8192 | bytes 65536 | tf_op jit(solution)/shard_map/while/body/eval_jaxpr/psum | solution.py:26
  542.8 11.7 %custom-call.15 = f32[2,64,64]{2,1,0:T(8,128)S(1)} custom-call(f32[2,64,64]{2,1,0:T(8,128)S(1)} %fusion.125), custom_call_target="Cholesky" | custom-call | tf_op jit(solution)/shard_map/while/body/eval_jaxpr/jit(cholesky)/cholesky | solution.py:10
  554.8 9.8 %custom-call.16 = f32[2,1,64,64]{2,3,1,0:T(8,128)S(1)} custom-call(f32[2,1,64,64]{3,2,1,0:T(8,128)S(1)} %select_bitcast_fusion.3), custom_call_target="InvertDiagBlocksLowerTriangular" | custom-call | tf_op jit(solution)/shard_map/while/body/eval_jaxpr/vmap(jit(_solve_triangular))/triangular_solve | solution.py:12
  567.1 7.5 all-reduce.15.cloned.1.call-done
  575.9 5.1 fusion.120
  585.7 35.3 %all-reduce.13.cloned.1.call-done = f32[2,16,64,64]{3,2,1,0:T(8,128)} async-done(((f32[2,16,64,64]{3,2,1,0:T(8,128)}), f32[2,16,64,64]{3,2,1,0:T(8,128)}) %all-reduce.13.cloned.1.call-update) | async-done | bytes 524304 | tf_op jit(solution)/shard_map/while/body/eval_jaxpr/psum | solution.py:23
  626.8 37.6 %psum.106 = f32[2,64,64]{1,2,0:T(8,128)S(1)} all-reduce(f32[2,64,64]{1,2,0:T(8,128)S(1)} %convolution_bitcast_fusion.10), channel_id=1, replica_groups=mesh['mode'=8,'rep'=4] {'mode'}, use_global_device_ids=true, to_apply=%region_12.14 | all-reduce | flops 8192 | bytes 65536 | tf_op jit(solution)/shard_map/while/body/eval_jaxpr/psum | solution.py:26
  664.5 11.7 %custom-call.15 = f32[2,64,64]{2,1,0:T(8,128)S(1)} custom-call(f32[2,64,64]{2,1,0:T(8,128)S(1)} %fusion.125), custom_call_target="Cholesky" | custom-call | tf_op jit(solution)/shard_map/while/body/eval_jaxpr/jit(cholesky)/cholesky | solution.py:10
  676.5 9.8 %custom-call.16 = f32[2,1,64,64]{2,3,1,0:T(8,128)S(1)} custom-call(f32[2,1,64,64]{3,2,1,0:T(8,128)S(1)} %select_bitcast_fusion.3), custom_call_target="InvertDiagBlocksLowerTriangular" | custom-call | tf_op jit(solution)/shard_map/while/body/eval_jaxpr/vmap(jit(_solve_triangular))/triangular_solve | solution.py:12
  688.8 7.5 all-reduce.15.cloned.1.call-done
  697.6 5.1 fusion.120
  707.4 35.3 %all-reduce.13.cloned.1.call-done = f32[2,16,64,64]{3,2,1,0:T(8,128)} async-done(((f32[2,16,64,64]{3,2,1,0:T(8,128)}), f32[2,16,64,64]{3,2,1,0:T(8,128)}) %all-reduce.13.cloned.1.call-update) | async-done | bytes 524304 | tf_op jit(solution)/shard_map/while/body/eval_jaxpr/psum | solution.py:23
  748.5 37.6 %psum.106 = f32[2,64,64]{1,2,0:T(8,128)S(1)} all-reduce(f32[2,64,64]{1,2,0:T(8,128)S(1)} %convolution_bitcast_fusion.10), channel_id=1, replica_groups=mesh['mode'=8,'rep'=4] {'mode'}, use_global_device_ids=true, to_apply=%region_12.14 | all-reduce | flops 8192 | bytes 65536 | tf_op jit(solution)/shard_map/while/body/eval_jaxpr/psum | solution.py:26
  786.2 11.7 %custom-call.15 = f32[2,64,64]{2,1,0:T(8,128)S(1)} custom-call(f32[2,64,64]{2,1,0:T(8,128)S(1)} %fusion.125), custom_call_target="Cholesky" | custom-call | tf_op jit(solution)/shard_map/while/body/eval_jaxpr/jit(cholesky)/cholesky | solution.py:10
  798.2 9.8 %custom-call.16 = f32[2,1,64,64]{2,3,1,0:T(8,128)S(1)} custom-call(f32[2,1,64,64]{3,2,1,0:T(8,128)S(1)} %select_bitcast_fusion.3), custom_call_target="InvertDiagBlocksLowerTriangular" | custom-call | tf_op jit(solution)/shard_map/while/body/eval_jaxpr/vmap(jit(_solve_triangular))/triangular_solve | solution.py:12
  810.5 7.5 all-reduce.15.cloned.1.call-done
  819.5 10.7 %psum.98 = f32[2,16,64]{2,1,0:T(8,128)} all-reduce(f32[2,16,64]{2,1,0:T(8,128)S(1)} %convolution_bitcast_fusion.4), channel_id=1, replica_groups=mesh['mode'=8,'rep'=4] {'rep'}, use_global_device_ids=true, to_apply=%region_14.17 | all-reduce | flops 2048 | bytes 16384 | tf_op jit(solution)/shard_map/psum | solution.py:81
  (142 shorter events, 68.6 us)
Async XLA Ops:
  7.2 308.2 %copy-start = (f32[2,2,16,64]{3,2,1,0:T(8,128)S(1)}, f32[2,2,16,64]{3,2,1,0:T(8,128)}, u32[]{:S(2)}) copy-start(f32[2,2,16,64]{3,2,1,0:T(8,128)} %param.15) | copy-start | bytes 49156
  7.2 77.3 %all-reduce.7.cloned.1.call-start = ((), (), s32[]{:S(2)}) async-start(), calls=%async_computation | async-start | bytes 262144 | tf_op jit(solution)/shard_map/psum | solution.py:18
  9.8 6.2 copy-start.4
  85.4 75.7 %all-reduce.11.cloned.1.call-start = ((), (), s32[]{:S(2)}) async-start(), calls=%async_computation.2 | async-start | bytes 262144 | tf_op jit(solution)/shard_map/while/body/eval_jaxpr/psum | solution.py:18
  162.1 75.7 %all-reduce.11.cloned.1.call-start = ((), (), s32[]{:S(2)}) async-start(), calls=%async_computation.2 | async-start | bytes 262144 | tf_op jit(solution)/shard_map/while/body/eval_jaxpr/psum | solution.py:18
  238.7 75.7 %all-reduce.11.cloned.1.call-start = ((), (), s32[]{:S(2)}) async-start(), calls=%async_computation.2 | async-start | bytes 262144 | tf_op jit(solution)/shard_map/while/body/eval_jaxpr/psum | solution.py:18
  315.3 137.3 %all-reduce.9.cloned.1.call-start = ((), (), s32[]{:S(2)}) async-start(), calls=%async_computation.1 | async-start | bytes 262144 | tf_op jit(solution)/shard_map/psum | solution.py:26
  453.9 365.3 %copy-start.5 = (f32[2,2,16,64]{3,2,1,0:T(8,128)S(1)}, f32[2,2,16,64]{3,2,1,0:T(8,128)}, u32[]{:S(2)}) copy-start(f32[2,2,16,64]{3,2,1,0:T(8,128)} %param.17) | copy-start | bytes 49156
  454.1 5.2 copy-start.2
  454.1 45.2 %all-reduce.13.cloned.1.call-start = ((), (), s32[]{:S(2)}) async-start(), calls=%async_computation.3 | async-start | bytes 2097152 | tf_op jit(solution)/shard_map/while/body/eval_jaxpr/psum | solution.py:23
  463.8 110.8 %all-reduce.15.cloned.1.call-start = ((), (), s32[]{:S(2)}) async-start(), calls=%async_computation.4 | async-start | bytes 262144 | tf_op jit(solution)/shard_map/while/body/eval_jaxpr/psum | solution.py:26
  499.3 3.9 copy-start.1
  565.9 9.9 %copy-start.3 = (f32[4,2,2,64,64]{4,3,2,1,0:T(8,128)S(1)}, f32[4,2,2,64,64]{4,3,2,1,0:T(8,128)}, u32[]{:S(2)}) copy-start(f32[4,2,2,64,64]{4,3,2,1,0:T(8,128)} %copy-done.2) | copy-start | bytes 786436 | tf_op jit(solution)/shard_map/while
  575.8 5.2 copy-start.2
  575.8 45.2 %all-reduce.13.cloned.1.call-start = ((), (), s32[]{:S(2)}) async-start(), calls=%async_computation.3 | async-start | bytes 2097152 | tf_op jit(solution)/shard_map/while/body/eval_jaxpr/psum | solution.py:23
  585.5 110.8 %all-reduce.15.cloned.1.call-start = ((), (), s32[]{:S(2)}) async-start(), calls=%async_computation.4 | async-start | bytes 262144 | tf_op jit(solution)/shard_map/while/body/eval_jaxpr/psum | solution.py:26
  621.0 3.9 copy-start.1
  687.6 9.9 %copy-start.3 = (f32[4,2,2,64,64]{4,3,2,1,0:T(8,128)S(1)}, f32[4,2,2,64,64]{4,3,2,1,0:T(8,128)}, u32[]{:S(2)}) copy-start(f32[4,2,2,64,64]{4,3,2,1,0:T(8,128)} %copy-done.2) | copy-start | bytes 786436 | tf_op jit(solution)/shard_map/while
  697.5 5.2 copy-start.2
  697.6 45.2 %all-reduce.13.cloned.1.call-start = ((), (), s32[]{:S(2)}) async-start(), calls=%async_computation.3 | async-start | bytes 2097152 | tf_op jit(solution)/shard_map/while/body/eval_jaxpr/psum | solution.py:23
  707.2 110.8 %all-reduce.15.cloned.1.call-start = ((), (), s32[]{:S(2)}) async-start(), calls=%async_computation.4 | async-start | bytes 262144 | tf_op jit(solution)/shard_map/while/body/eval_jaxpr/psum | solution.py:26
  742.7 3.9 copy-start.1
  809.3 9.9 %copy-start.3 = (f32[4,2,2,64,64]{4,3,2,1,0:T(8,128)S(1)}, f32[4,2,2,64,64]{4,3,2,1,0:T(8,128)}, u32[]{:S(2)}) copy-start(f32[4,2,2,64,64]{4,3,2,1,0:T(8,128)} %copy-done.2) | copy-start | bytes 786436 | tf_op jit(solution)/shard_map/while
Sparse Core Ops, SparseCore 0:
  11.3 73.0 all-reduce.6
  91.6 69.4 all-reduce.10
  168.3 69.4 all-reduce.10
  244.9 69.4 all-reduce.10
  384.8 67.7 all-reduce.8
  463.9 35.3 all-reduce.12
  503.3 71.2 all-reduce.14
  585.6 35.3 all-reduce.12
  625.0 71.2 all-reduce.14
  707.3 35.3 all-reduce.12
  746.7 71.2 all-reduce.14
where the time goes:
time: 838 us; the launch traced here: 837 us
  waiting for transfers between devices  472 us (56%)
  blocking collectives  169 us (20%)
  other arithmetic  91.9 us (11%)
  matrix products  77.3 us (9%)
  between operations  13.9 us (2%)
  local copies, waits for them, and re-layouts  11.1 us (1%)
    psum x4, waiting for transfers between devices, sketch_total(): return lax.psum(partial_value, 'mode')  277 us
    psum x4, blocking collectives, orthogonal(): gram_total, raw_total = lax.psum((gram_part, raw_part), 'mode')  148 us
    psum x3, waiting for transfers between devices, orthogonal(): mixture = lax.psum(local_mix, 'rep')  106 us
    psum x4, waiting for transfers between devices, orthogonal(): gram_total, raw_total = lax.psum((gram_part, raw_part), 'mode')  89.3 us
    another operation x16, other arithmetic, lower_inverse(): factor = jnp.linalg.cholesky(gram_matrix)  47.6 us
    another operation x12, other arithmetic, lower_inverse(): jax.scipy.linalg.solve_triangular(single, identity, lower=True)  39.7 us
  transfers between devices with their start and end apart: 11, of which 11 were waited for; matrix products, arithmetic and copies ran while one was open for 11% of the time, Pallas kernels for 0%

commit v1 on v0

--- a/solution.py
+++ b/solution.py
@@ -15,7 +15,7 @@
 
 
 def sketch_total(partial_value):
-    return lax.psum(partial_value, "mode")
+    return jnp.sum(lax.all_gather(partial_value, "mode"), axis=0)
 
 
 def orthogonal(pieces, sketch, bond_mask, row_count):

time: 838 us -> 635 us (0.76)
  waiting for transfers between devices: 472 us -> 139 us
  blocking collectives: 169 us -> 305 us
    psum x4 -> x0, waiting for transfers between devices: 277 us -> none  [sketch_total(): return lax.psum(partial_value, 'mode')]
    all_gather x0 -> x4, blocking collectives: none -> 135 us  [sketch_total(): return jnp.sum(lax.all_gather(partial_value, 'mode'), axis=0)]
    psum x4, waiting for transfers between devices: 89.3 us -> 33.1 us  [orthogonal(): gram_total, raw_total = lax.psum((gram_part, raw_part), 'mode')]
  transfers between devices with their start and end apart: 11 -> 7, of which waited for: 11 -> 7; matrix products, arithmetic and copies ran while one was open for 11% -> 16% of each run, Pallas kernels for 0% -> 0%
where the time goes in v1:
time: 635 us; the launch traced here: 634 us
  blocking collectives  305 us (48%)
  waiting for transfers between devices  139 us (22%)
  other arithmetic  88.6 us (14%)
  matrix products  74.7 us (12%)
  between operations  14.2 us (2%)
  local copies, waits for them, and re-layouts  11.1 us (2%)
    psum x4, blocking collectives, orthogonal(): gram_total, raw_total = lax.psum((gram_part, raw_part), 'mode')  149 us
    all_gather x4, blocking collectives, sketch_total(): return jnp.sum(lax.all_gather(partial_value, 'mode'), axis=0)  135 us
    psum x3, waiting for transfers between devices, orthogonal(): mixture = lax.psum(local_mix, 'rep')  106 us
    another operation x16, other arithmetic, lower_inverse(): factor = jnp.linalg.cholesky(gram_matrix)  47.6 us
    another operation x12, other arithmetic, lower_inverse(): jax.scipy.linalg.solve_triangular(single, identity, lower=True)  39.7 us
    psum x4, waiting for transfers between devices, orthogonal(): gram_total, raw_total = lax.psum((gram_part, raw_part), 'mode')  33.1 us
    dot_general x3, matrix products, left_step(): jnp.einsum('bsac,bsicd->bsiad', carried_now, core_now, precision=PRECISE)  15.4 us
    dot_general x4, matrix products, orthogonal(): jnp.einsum('bsiad,bsde->biae', pieces, sketch, precision=PRECISE)  13.5 us
  transfers between devices with their start and end apart: 7, of which 7 were waited for; matrix products, arithmetic and copies ran while one was open for 16% of the time, Pallas kernels for 0%

profile of v1, /device:TPU:0, one launch (start us, length us, event | category | flops | bytes accessed | tf_op | source)
XLA Modules:
  0.0 634.1 jit_solution(9243314291509698856)
XLA Ops:
  8.4 34.6 %all-gather.1 = f32[16,2,64,64]{3,2,1,0:T(8,128)S(1)} all-gather(f32[2,2,64,64]{3,2,1,0:T(8,128)S(1)} %fusion.49), channel_id=3, replica_groups=mesh['mode'=8,'rep'=4] {'mode'}, dimensions={0}, use_global_device_ids=true | all-gather | bytes 589824 | tf_op jit(solution)/shard_map/all_gather | solution.py:18
  43.9 6.2 reshape.165
  50.7 116.5 %while.35 = (s32[]{:T(128)}, f32[4,2,2,64,64]{4,3,2,1,0:T(8,128)S(1)}, f32[2,2,3,16,64,64]{5,4,3,2,1,0:T(8,128)}, f32[3,16,64,64]{3,2,1,0:T(8,128)S(1)}, f32[4,6...) while((s32[]{:T(128)}, ...), condition=%wide.region_3.4_spmd, body=%wide.region_1.3_spmd.sunk | while | flops 402784256 | bytes 7406866 | solution.py:60
  56.1 33.3 %all-gather.3 = f32[16,2,64,64]{3,2,1,0:T(8,128)S(1)} all-gather(f32[2,2,64,64]{3,2,1,0:T(8,128)S(1)} %convolution_bitcast_fusion.9), channel_id=2, replica_groups=mesh['mode'=8,'rep'=4] {'mode'}, dimensions={0}, use_global_device_ids=true | all-gather | bytes 589824 | tf_op jit(solution)/shard_map/while/body/eval_jaxpr/all_gather | solution.py:18
  94.8 34.2 %all-gather.3 = f32[16,2,64,64]{3,2,1,0:T(8,128)S(1)} all-gather(f32[2,2,64,64]{3,2,1,0:T(8,128)S(1)} %convolution_bitcast_fusion.9), channel_id=2, replica_groups=mesh['mode'=8,'rep'=4] {'mode'}, dimensions={0}, use_global_device_ids=true | all-gather | bytes 589824 | tf_op jit(solution)/shard_map/while/body/eval_jaxpr/all_gather | solution.py:18
  134.5 32.6 %all-gather.3 = f32[16,2,64,64]{3,2,1,0:T(8,128)S(1)} all-gather(f32[2,2,64,64]{3,2,1,0:T(8,128)S(1)} %convolution_bitcast_fusion.9), channel_id=2, replica_groups=mesh['mode'=8,'rep'=4] {'mode'}, dimensions={0}, use_global_device_ids=true | all-gather | bytes 589824 | tf_op jit(solution)/shard_map/while/body/eval_jaxpr/all_gather | solution.py:18
  167.5 10.1 %psum.70 = f32[2,16,64]{2,1,0:T(8,128)S(1)} all-reduce(f32[2,16,64]{2,1,0:T(8,128)S(1)} %convolution_bitcast_fusion.5), channel_id=1, replica_groups=mesh['mode'=8,'rep'=4] {'rep'}, use_global_device_ids=true, to_apply=%region_4.5 | all-reduce | flops 2048 | bytes 16384 | tf_op jit(solution)/shard_map/psum | solution.py:23
  178.9 36.7 %psum.71 = f32[2,64,64]{1,2,0:T(8,128)S(1)} all-reduce(f32[2,64,64]{1,2,0:T(8,128)S(1)} %fusion.53), channel_id=1, replica_groups=mesh['mode'=8,'rep'=4] {'mode'}, use_global_device_ids=true, to_apply=%region_5.6 | all-reduce | flops 8192 | bytes 65536 | tf_op jit(solution)/shard_map/psum | solution.py:26
  215.8 11.7 %custom-call.10 = f32[2,64,64]{2,1,0:T(8,128)S(1)} custom-call(f32[2,64,64]{2,1,0:T(8,128)S(1)} %fusion.44), custom_call_target="Cholesky" | custom-call | tf_op jit(solution)/shard_map/jit(cholesky)/cholesky | solution.py:10
  227.8 9.8 %custom-call.11 = f32[2,1,64,64]{2,3,1,0:T(8,128)S(1)} custom-call(f32[2,1,64,64]{3,2,1,0:T(8,128)S(1)} %select_bitcast_fusion.1), custom_call_target="InvertDiagBlocksLowerTriangular" | custom-call | tf_op jit(solution)/shard_map/vmap(jit(_solve_triangular))/triangular_solve | solution.py:12
  238.8 10.7 %all-reduce.5.cloned.1.call-done = f32[2,2,64,64]{3,2,1,0:T(8,128)} async-done(((f32[2,2,64,64]{3,2,1,0:T(8,128)}), f32[2,2,64,64]{3,2,1,0:T(8,128)}) %all-reduce.5.cloned.1.call-update) | async-done | bytes 65552 | tf_op jit(solution)/shard_map/psum | solution.py:26
  250.8 365.5 %while.36 = (s32[]{:T(128)}, f32[2,2,64,64]{2,3,1,0:T(8,128)S(1)}, f32[2,3,16,4096]{3,2,1,0:T(8,128)}, f32[2,2,3,16,64,64]{5,4,3,2,1,0:T(8,128)}, f32[4,2,2,64,6...) while((s32[]{:T(128)}, f32[2,2,64,64]{2,3,1,0:T(8,128)S(1)}, ...), condition=%wide.region_13.16_spmd, body=%wide.region_9.15_spmd.sunk | while | flops 824467648 | bytes 21006400 | solution.py:79
  251.1 5.1 fusion.123
  256.2 4.4 fusion.124
  260.9 35.5 %all-reduce.7.cloned.1.call-done = f32[2,16,64,64]{3,2,1,0:T(8,128)} async-done(((f32[2,16,64,64]{3,2,1,0:T(8,128)}), f32[2,16,64,64]{3,2,1,0:T(8,128)}) %all-reduce.7.cloned.1.call-update) | async-done | bytes 524304 | tf_op jit(solution)/shard_map/while/body/eval_jaxpr/psum | solution.py:23
  302.2 37.6 %psum.79 = f32[2,64,64]{1,2,0:T(8,128)S(1)} all-reduce(f32[2,64,64]{1,2,0:T(8,128)S(1)} %convolution_bitcast_fusion.10), channel_id=1, replica_groups=mesh['mode'=8,'rep'=4] {'mode'}, use_global_device_ids=true, to_apply=%region_12.14 | all-reduce | flops 8192 | bytes 65536 | tf_op jit(solution)/shard_map/while/body/eval_jaxpr/psum | solution.py:26
  339.8 11.7 %custom-call.15 = f32[2,64,64]{2,1,0:T(8,128)S(1)} custom-call(f32[2,64,64]{2,1,0:T(8,128)S(1)} %fusion.128), custom_call_target="Cholesky" | custom-call | tf_op jit(solution)/shard_map/while/body/eval_jaxpr/jit(cholesky)/cholesky | solution.py:10
  351.8 9.8 %custom-call.16 = f32[2,1,64,64]{2,3,1,0:T(8,128)S(1)} custom-call(f32[2,1,64,64]{3,2,1,0:T(8,128)S(1)} %select_bitcast_fusion.3), custom_call_target="InvertDiagBlocksLowerTriangular" | custom-call | tf_op jit(solution)/shard_map/while/body/eval_jaxpr/vmap(jit(_solve_triangular))/triangular_solve | solution.py:12
  364.2 7.5 %all-reduce.9.cloned.1.call-done = f32[2,2,64,64]{2,3,1,0:T(8,128)} async-done(((f32[2,2,64,64]{2,3,1,0:T(8,128)}), f32[2,2,64,64]{2,3,1,0:T(8,128)}) %all-reduce.9.cloned.1.call-update) | async-done | bytes 65552 | tf_op jit(solution)/shard_map/while/body/eval_jaxpr/psum | solution.py:26
  373.0 5.1 fusion.123
  382.8 35.3 %all-reduce.7.cloned.1.call-done = f32[2,16,64,64]{3,2,1,0:T(8,128)} async-done(((f32[2,16,64,64]{3,2,1,0:T(8,128)}), f32[2,16,64,64]{3,2,1,0:T(8,128)}) %all-reduce.7.cloned.1.call-update) | async-done | bytes 524304 | tf_op jit(solution)/shard_map/while/body/eval_jaxpr/psum | solution.py:23
  423.9 37.6 %psum.79 = f32[2,64,64]{1,2,0:T(8,128)S(1)} all-reduce(f32[2,64,64]{1,2,0:T(8,128)S(1)} %convolution_bitcast_fusion.10), channel_id=1, replica_groups=mesh['mode'=8,'rep'=4] {'mode'}, use_global_device_ids=true, to_apply=%region_12.14 | all-reduce | flops 8192 | bytes 65536 | tf_op jit(solution)/shard_map/while/body/eval_jaxpr/psum | solution.py:26
  461.6 11.7 %custom-call.15 = f32[2,64,64]{2,1,0:T(8,128)S(1)} custom-call(f32[2,64,64]{2,1,0:T(8,128)S(1)} %fusion.128), custom_call_target="Cholesky" | custom-call | tf_op jit(solution)/shard_map/while/body/eval_jaxpr/jit(cholesky)/cholesky | solution.py:10
  473.5 9.8 %custom-call.16 = f32[2,1,64,64]{2,3,1,0:T(8,128)S(1)} custom-call(f32[2,1,64,64]{3,2,1,0:T(8,128)S(1)} %select_bitcast_fusion.3), custom_call_target="InvertDiagBlocksLowerTriangular" | custom-call | tf_op jit(solution)/shard_map/while/body/eval_jaxpr/vmap(jit(_solve_triangular))/triangular_solve | solution.py:12
  485.9 7.5 %all-reduce.9.cloned.1.call-done = f32[2,2,64,64]{2,3,1,0:T(8,128)} async-done(((f32[2,2,64,64]{2,3,1,0:T(8,128)}), f32[2,2,64,64]{2,3,1,0:T(8,128)}) %all-reduce.9.cloned.1.call-update) | async-done | bytes 65552 | tf_op jit(solution)/shard_map/while/body/eval_jaxpr/psum | solution.py:26
  494.7 5.1 fusion.123
  504.5 35.3 %all-reduce.7.cloned.1.call-done = f32[2,16,64,64]{3,2,1,0:T(8,128)} async-done(((f32[2,16,64,64]{3,2,1,0:T(8,128)}), f32[2,16,64,64]{3,2,1,0:T(8,128)}) %all-reduce.7.cloned.1.call-update) | async-done | bytes 524304 | tf_op jit(solution)/shard_map/while/body/eval_jaxpr/psum | solution.py:23
  545.5 37.6 %psum.79 = f32[2,64,64]{1,2,0:T(8,128)S(1)} all-reduce(f32[2,64,64]{1,2,0:T(8,128)S(1)} %convolution_bitcast_fusion.10), channel_id=1, replica_groups=mesh['mode'=8,'rep'=4] {'mode'}, use_global_device_ids=true, to_apply=%region_12.14 | all-reduce | flops 8192 | bytes 65536 | tf_op jit(solution)/shard_map/while/body/eval_jaxpr/psum | solution.py:26
  583.2 11.7 %custom-call.15 = f32[2,64,64]{2,1,0:T(8,128)S(1)} custom-call(f32[2,64,64]{2,1,0:T(8,128)S(1)} %fusion.128), custom_call_target="Cholesky" | custom-call | tf_op jit(solution)/shard_map/while/body/eval_jaxpr/jit(cholesky)/cholesky | solution.py:10
  595.2 9.8 %custom-call.16 = f32[2,1,64,64]{2,3,1,0:T(8,128)S(1)} custom-call(f32[2,1,64,64]{3,2,1,0:T(8,128)S(1)} %select_bitcast_fusion.3), custom_call_target="InvertDiagBlocksLowerTriangular" | custom-call | tf_op jit(solution)/shard_map/while/body/eval_jaxpr/vmap(jit(_solve_triangular))/triangular_solve | solution.py:12
  607.6 7.5 %all-reduce.9.cloned.1.call-done = f32[2,2,64,64]{2,3,1,0:T(8,128)} async-done(((f32[2,2,64,64]{2,3,1,0:T(8,128)}), f32[2,2,64,64]{2,3,1,0:T(8,128)}) %all-reduce.9.cloned.1.call-update) | async-done | bytes 65552 | tf_op jit(solution)/shard_map/while/body/eval_jaxpr/psum | solution.py:26
  616.6 10.7 %psum.73 = f32[2,16,64]{2,1,0:T(8,128)} all-reduce(f32[2,16,64]{2,1,0:T(8,128)S(1)} %convolution_bitcast_fusion.4), channel_id=1, replica_groups=mesh['mode'=8,'rep'=4] {'rep'}, use_global_device_ids=true, to_apply=%region_14.17 | all-reduce | flops 2048 | bytes 16384 | tf_op jit(solution)/shard_map/psum | solution.py:81
  (138 shorter events, 62.5 us)
Async XLA Ops:
  7.2 160.1 %copy-start = (f32[2,2,16,64]{3,2,1,0:T(8,128)S(1)}, f32[2,2,16,64]{3,2,1,0:T(8,128)}, u32[]{:S(2)}) copy-start(f32[2,2,16,64]{3,2,1,0:T(8,128)} %param.15) | copy-start | bytes 49156
  7.2 242.3 %all-reduce.5.cloned.1.call-start = ((), (), s32[]{:S(2)}) async-start(), calls=%async_computation | async-start | bytes 262144 | tf_op jit(solution)/shard_map/psum | solution.py:26
  43.9 6.2 copy-start.4
  250.8 365.5 %copy-start.5 = (f32[2,2,16,64]{3,2,1,0:T(8,128)S(1)}, f32[2,2,16,64]{3,2,1,0:T(8,128)}, u32[]{:S(2)}) copy-start(f32[2,2,16,64]{3,2,1,0:T(8,128)} %param.17) | copy-start | bytes 49156
  251.0 5.2 copy-start.2
  251.0 45.4 %all-reduce.7.cloned.1.call-start = ((), (), s32[]{:S(2)}) async-start(), calls=%async_computation.1 | async-start | bytes 2097152 | tf_op jit(solution)/shard_map/while/body/eval_jaxpr/psum | solution.py:23
  260.7 111.0 %all-reduce.9.cloned.1.call-start = ((), (), s32[]{:S(2)}) async-start(), calls=%async_computation.2 | async-start | bytes 262144 | tf_op jit(solution)/shard_map/while/body/eval_jaxpr/psum | solution.py:26
  296.4 3.9 copy-start.1
  363.0 9.9 %copy-start.3 = (f32[4,2,2,64,64]{4,3,2,1,0:T(8,128)S(1)}, f32[4,2,2,64,64]{4,3,2,1,0:T(8,128)}, u32[]{:S(2)}) copy-start(f32[4,2,2,64,64]{4,3,2,1,0:T(8,128)} %copy-done.2) | copy-start | bytes 786436 | tf_op jit(solution)/shard_map/while
  372.9 5.2 copy-start.2
  372.9 45.2 %all-reduce.7.cloned.1.call-start = ((), (), s32[]{:S(2)}) async-start(), calls=%async_computation.1 | async-start | bytes 2097152 | tf_op jit(solution)/shard_map/while/body/eval_jaxpr/psum | solution.py:23
  382.6 110.8 %all-reduce.9.cloned.1.call-start = ((), (), s32[]{:S(2)}) async-start(), calls=%async_computation.2 | async-start | bytes 262144 | tf_op jit(solution)/shard_map/while/body/eval_jaxpr/psum | solution.py:26
  418.1 3.9 copy-start.1
  484.7 9.9 %copy-start.3 = (f32[4,2,2,64,64]{4,3,2,1,0:T(8,128)S(1)}, f32[4,2,2,64,64]{4,3,2,1,0:T(8,128)}, u32[]{:S(2)}) copy-start(f32[4,2,2,64,64]{4,3,2,1,0:T(8,128)} %copy-done.2) | copy-start | bytes 786436 | tf_op jit(solution)/shard_map/while
  494.6 5.2 copy-start.2
  494.6 45.1 %all-reduce.7.cloned.1.call-start = ((), (), s32[]{:S(2)}) async-start(), calls=%async_computation.1 | async-start | bytes 2097152 | tf_op jit(solution)/shard_map/while/body/eval_jaxpr/psum | solution.py:23
  504.3 110.8 %all-reduce.9.cloned.1.call-start = ((), (), s32[]{:S(2)}) async-start(), calls=%async_computation.2 | async-start | bytes 262144 | tf_op jit(solution)/shard_map/while/body/eval_jaxpr/psum | solution.py:26
  539.8 3.9 copy-start.1
  606.4 9.9 %copy-start.3 = (f32[4,2,2,64,64]{4,3,2,1,0:T(8,128)S(1)}, f32[4,2,2,64,64]{4,3,2,1,0:T(8,128)}, u32[]{:S(2)}) copy-start(f32[4,2,2,64,64]{4,3,2,1,0:T(8,128)} %copy-done.2) | copy-start | bytes 786436 | tf_op jit(solution)/shard_map/while
Sparse Core Ops, SparseCore 0:
  178.7 70.7 all-reduce.4
  260.8 35.5 all-reduce.6
  300.4 71.2 all-reduce.8
  382.7 35.3 all-reduce.6
  422.1 71.2 all-reduce.8
  504.4 35.3 all-reduce.6
  543.8 71.2 all-reduce.8
